TPU v7x, 256 devices: a whole 4x4x8 slice. The times are simulated.
256 devices in a mesh: node: 16 (over x, z_hi), tm: 16 (over z_lo, y, core).
Axes of the slice: x: 4, y: 4, z: 8 (z_hi: 4, z_lo: 2; z = z_hi * 2 + z_lo), core: 2. Of those that a mesh axis runs over, the one named last changes fastest.
Arguments:
- codes: int32 [65536, 2048], P('node', 'tm'), may hold values from -127 to 127
- node_scale: float32 [65536], P('node'), may hold values from 0.002 to 0.02
- basis: bfloat16 [65536, 128], P('node'), may hold values from -0.0234375 to 0.0234375
- regular: float32 [8384], replicated, may hold values from 0.05 to 0.5
- feature_order: int32 [8384], replicated, may hold values from 0 to 8383, each once
- panel_inverse: float32 [2, 262, 262], replicated, may hold values from -0.06 to 1.2
Outputs:
- schur: float32 [8384, 8384], P('node', 'tm')
Inputs may be any that keep to these rules, and one draw needn't show every extreme that they name: `feature_order`: a permutation: every feature stands at exactly one position.
All inputs are finite; a program needn't handle non-finite values.
Results may differ from a plain program's by a relative error of at most 0.0051.
Values sent between devices are 32-bit elements; how exact they have to be, the bound alone decides.
A program may use at most 64 MiB of HBM per device.

v0:
```python
import jax
import jax.numpy as jnp
import numpy as np
from jax import lax
from jax.sharding import PartitionSpec as P


def pair_starts(rank_count):
    leading = np.arange(rank_count + 1)
    return (leading * (rank_count + 1) - leading * (leading - 1) // 2).astype(np.int32)


def selectors(chosen, rank_count):
    starts = pair_starts(rank_count)
    modes = jnp.arange(rank_count, dtype=jnp.int32)
    below = chosen[:, None] >= jnp.asarray(starts[:-1])[None, :]
    above = chosen[:, None] < jnp.asarray(starts[1:])[None, :]
    lead = jnp.logical_and(below, above)
    shift = modes - jnp.asarray(starts[:-1])
    trailing = chosen + jnp.sum(jnp.where(lead, shift[None, :], 0), axis=1)
    trail = trailing[:, None] == modes[None, :]
    keep = (trailing < rank_count).astype(jnp.float32)
    return (lead.astype(jnp.bfloat16), trail.astype(jnp.bfloat16), 1.0 - keep)


def spread(values):
    high = lax.reduce_precision(values, 8, 7)
    low = lax.reduce_precision(values - high, 8, 7)
    return jnp.concatenate([high, low], axis=1).astype(jnp.bfloat16)


def make_features(pieces, picks):
    lead, trail, constant = picks
    dims = (((1,), (1,)), ((), ()))
    lead = jnp.concatenate([lead, lead], axis=1)
    trail = jnp.concatenate([trail, trail], axis=1)
    lead_vals = lax.dot_general(lead, pieces, dims, preferred_element_type=jnp.float32)
    trail_vals = lax.dot_general(trail, pieces, dims, preferred_element_type=jnp.float32)
    return (lead_vals * (trail_vals + constant[:, None])).astype(jnp.bfloat16)


def contract(left_feats, right_feats):
    return lax.dot_general(
        left_feats, right_feats, (((1,), (1,)), ((), ())), preferred_element_type=jnp.float32
    )


def highest(left_mat, right_mat):
    return jnp.dot(
        left_mat, right_mat, precision=lax.Precision.HIGHEST, preferred_element_type=jnp.float32
    )


def per_device(codes, node_scale, basis, regular, feature_order, panel_inverse):
    rank_count = basis.shape[1]
    snap_local = codes.shape[1]
    nfeat = regular.shape[0]
    row_size = nfeat // lax.axis_size("node")
    col_size = nfeat // lax.axis_size("tm")
    snap_total = snap_local * lax.axis_size("tm")
    panel_width = panel_inverse.shape[1]
    span = 2 * panel_width
    scaled_basis = (basis.astype(jnp.float32) * node_scale[:, None]).astype(jnp.bfloat16)
    code_values = codes.astype(jnp.bfloat16)
    row_offset = lax.axis_index("node") * row_size
    col_offset = lax.axis_index("tm") * col_size
    row_picks = selectors(lax.dynamic_slice_in_dim(feature_order, row_offset, row_size), rank_count)
    col_picks = selectors(lax.dynamic_slice_in_dim(feature_order, col_offset, col_size), rank_count)
    pan_picks = selectors(feature_order[:span], rank_count)
    summed = lax.psum(
        lax.dot_general(
            code_values, scaled_basis, (((0,), (0,)), ((), ())), preferred_element_type=jnp.float32
        ),
        "node",
    )
    pieces = spread(lax.all_gather(summed, "tm", axis=0, tiled=True))
    row_feats = make_features(pieces, row_picks)
    col_feats = make_features(pieces, col_picks)
    pan_feats = make_features(pieces, pan_picks)
    row_global = row_offset + jnp.arange(row_size, dtype=jnp.int32)
    col_global = col_offset + jnp.arange(col_size, dtype=jnp.int32)
    pan_global = jnp.arange(span, dtype=jnp.int32)
    row_regular = lax.dynamic_slice_in_dim(regular, row_offset, row_size)

    def block(left_feats, right_feats, left_global, right_global, left_regular):
        same = (left_global[:, None] == right_global[None, :]).astype(jnp.float32)
        return contract(left_feats, right_feats) / snap_total + same * left_regular[:, None]

    matrix = block(row_feats, col_feats, row_global, col_global, row_regular)
    left = block(row_feats, pan_feats, row_global, pan_global, row_regular)
    upper = block(pan_feats, col_feats, pan_global, col_global, regular[:span])
    w = panel_width
    inner = contract(pan_feats[:w], pan_feats[w:]) / snap_total
    first_left = highest(left[:, :w], panel_inverse[0])
    second_left = left[:, w:] - highest(first_left, inner)
    cross = highest(panel_inverse[0], inner)
    second_upper = upper[w:] - highest(cross.T, upper[:w])
    second_left = highest(second_left, panel_inverse[1])
    joint = jnp.concatenate([first_left, second_left], axis=1)
    return matrix - highest(joint, jnp.concatenate([upper[:w], second_upper], axis=0))


def solution(mesh):
    placed = (P("node", "tm"), P("node"), P("node", None), P(), P(), P())
    return jax.shard_map(
        per_device, mesh=mesh, in_specs=placed, out_specs=P("node", "tm"), check_vma=False
    )
```

profile of v0, /device:TPU:1, one launch (start us, length us, event | category | flops | bytes accessed | tf_op | source)
XLA Modules:
  0.0 236.5 jit_solution(14011582777847682140)
XLA Ops:
  6.5 0.0 copy-start.1
  6.5 0.0 copy-start.2
  6.5 0.0 copy-start.3
  6.5 0.0 copy-start
  6.5 0.0 all-reduce.2.cloned.1.call-start
  6.6 3.7 %convolution_bitcast_fusion = f32[128,128]{0,1:T(8,128)} fusion(bf16[4096,128]{1,0:T(8,128)(2,1)} %param.17, s32[4096,128]{1,0:T(8,128)} %param.15, f32[4096]{0:T(1024)} %param.16), kind=kOutput, calls=%fused_computation.24 | convolution fusion | flops 136314880 | bytes 3227648 | tf_op jit(solution)/shard_map/dot_general | solution.py:71
  10.3 0.0 all-reduce.2.cloned.1.call-update
  10.3 0.0 all-gather.2.cloned.1.call-start
  10.4 0.9 fusion.50
  11.3 147.1 %all-reduce.2.cloned.1.call-done = f32[128,128]{0,1:T(8,128)} async-done(((f32[128,128]{0,1:T(8,128)}), f32[128,128]{0,1:T(8,128)}) %all-reduce.2.cloned.1.call-update) | async-done | bytes 65552 | tf_op jit(solution)/shard_map/psum | solution.py:70
  158.3 0.0 all-gather.2.cloned.1.call-update
  158.3 0.0 copy-done.1
  158.3 0.0 copy-done.2
  158.4 0.0 copy-done.3
  158.4 0.6 select_reduce_fusion
  159.0 0.9 fusion.49
  159.8 0.7 convert_subtract_fusion
  160.5 0.1 iota_compare_fusion.4
  160.6 0.1 iota_compare_fusion.3
  160.8 0.1 iota_compare_fusion.2
  160.9 0.3 compare_and_fusion
  161.2 0.0 copy-done
  161.2 0.6 fusion.48
  161.9 41.1 %all-gather.2.cloned.1.call-done = f32[2048,128]{0,1:T(8,128)} async-done(((f32[128,128]{0,1:T(8,128)}), f32[2048,128]{0,1:T(8,128)}) %all-gather.2.cloned.1.call-update) | async-done | bytes 1048592 | tf_op jit(solution)/shard_map/all_gather | solution.py:76
  202.9 1.4 reduce-precision_convert_fusion
  204.3 0.7 fusion.17
  205.1 0.7 fusion.24
  205.8 0.7 fusion.31
  206.5 0.9 multiply_convert_fusion
  207.4 0.8 convolution_multiply_fusion.3
  208.2 0.8 multiply_convert_fusion.2
  209.0 2.0 fusion.1
  211.0 1.6 fusion.15
  212.6 1.9 fusion.39
  214.5 2.2 convolution_subtract_fusion.1
  216.7 0.8 multiply_convert_fusion.1
  217.5 1.9 fusion
  219.4 1.9 fusion.2
  221.3 1.5 convolution_subtract_fusion.2
  222.8 1.6 fusion.38
  224.4 5.2 %convolution_subtract_fusion = f32[524,524]{1,0:T(8,128)} fusion(f32[524,524]{1,0:T(8,128)S(1)} %fusion, f32[524,262]{0,1:T(8,128)S(1)} %fusion.38, f32[524,262]{0,1:T(8,128)S(1)} %fusion.15, f32[262,524]{1,0:T(8,128)S(1)} %convolution_subtract_fusion.2, f32[262,524]{1,0:T(8,128)S(1)} %slice.46), kind=kOutput, calls=%fused_computation.6 | convolution fusion | flops 1727357696 | bytes 4393216 | tf_op jit(solution)/shard_map/dot_general | solution.py:49
  (3 shorter events, 0.1 us)
Async XLA Ops:
  6.5 151.8 %copy-start.1 = (s32[128]{0:T(128)S(1)}, s32[128]{0:T(128)}, u32[]{:S(2)}) copy-start(s32[128]{0:T(128)} %constant.33.clone) | copy-start | bytes 1540
  6.5 151.8 %copy-start.2 = (s32[128]{0:T(128)S(1)}, s32[128]{0:T(128)}, u32[]{:S(2)}) copy-start(s32[128]{0:T(128)} %constant.32.clone) | copy-start | bytes 1540
  6.5 151.8 %copy-start.3 = (s32[128]{0:T(128)S(1)}, s32[128]{0:T(128)}, u32[]{:S(2)}) copy-start(s32[128]{0:T(128)} %constant.35) | copy-start | bytes 1540
  6.5 154.7 %copy-start = (f32[2,262,262]{2,0,1:T(2,128)S(1)}, f32[2,262,262]{2,0,1:T(2,128)}, u32[]{:S(2)}) copy-start(f32[2,262,262]{2,0,1:T(2,128)} %param.20) | copy-start | bytes 1647460
  6.5 151.8 %all-reduce.2.cloned.1.call-start = ((), (), s32[]{:S(2)}) async-start(), calls=%async_computation | async-start | bytes 131072 | tf_op jit(solution)/shard_map/psum | solution.py:70
  10.3 192.6 %all-gather.2.cloned.1.call-start = ((), (), s32[]{:S(2)}) async-start(), calls=%async_computation.1 | async-start | bytes 1114112 | tf_op jit(solution)/shard_map/all_gather | solution.py:76
Sparse Core Ops, SparseCore 0:
  10.4 147.8 all-reduce.1
  160.2 42.6 all-gather.1
where the time goes:
time: 237 us; the launch traced here: 236 us
  waiting for transfers between devices  188 us (79%)
  matrix products  28.9 us (12%)
  between operations  13.6 us (6%)
  other arithmetic  3.34 us (1%)
  local copies, waits for them, and re-layouts  2.42 us (1%)
    psum x1, waiting for transfers between devices, per_device(): lax.psum(lax.dot_general(code_values, scaled_basis, (((0,), (0,)), ((), (...  147 us
    all_gather x1, waiting for transfers between devices, per_device(): pieces = spread(lax.all_gather(summed, 'tm', axis=0, tiled=True))  41.1 us
    dot_general x6, matrix products, highest(): jnp.dot(left_mat, right_mat, precision=lax.Precision.HIGHEST, preferred_e...  14 us
    dot_general x4, matrix products, contract(): lax.dot_general(left_feats, right_feats, (((1,), (1,)), ((), ())), prefer...  6.5 us
  transfers between devices with their start and end apart: 2, of which 2 were waited for; matrix products, arithmetic and copies ran while one was open for 2% of the time, Pallas kernels for 0%

commit v1 on v0

--- a/solution.py
+++ b/solution.py
@@ -73,7 +73,11 @@
         ),
         "node",
     )
-    pieces = spread(lax.all_gather(summed, "tm", axis=0, tiled=True))
+    pieces = spread(
+        jnp.concatenate(
+            lax.all_to_all(jnp.stack([summed] * lax.axis_size("tm")), "tm", 0, 0), axis=0
+        )
+    )
     row_feats = make_features(pieces, row_picks)
     col_feats = make_features(pieces, col_picks)
     pan_feats = make_features(pieces, pan_picks)

time: 237 us -> 224 us (0.945)
  waiting for transfers between devices: 188 us -> 159 us
  starting transfers between devices: 0.08 us -> 14.9 us
    all_gather x1 -> x0, waiting for transfers between devices: 41.1 us -> none  [per_device(): pieces = spread(lax.all_gather(summed, 'tm', axis=0, tiled=True))]
    all_to_all x0 -> x1, starting transfers between devices: none -> 14.9 us  [per_device(): lax.all_to_all(jnp.stack([summed] * lax.axis_size('tm')), 'tm', 0, 0)]
    all_to_all x0 -> x1, waiting for transfers between devices: none -> 12.3 us  [per_device(): lax.all_to_all(jnp.stack([summed] * lax.axis_size('tm')), 'tm', 0, 0)]
where the time goes in v1:
time: 224 us; the launch traced here: 223 us
  waiting for transfers between devices  159 us (71%)
  matrix products  28.8 us (13%)
  starting transfers between devices  14.9 us (7%)
  between operations  13.6 us (6%)
  local copies, waits for them, and re-layouts  4.42 us (2%)
    psum x1, waiting for transfers between devices, per_device(): lax.psum(lax.dot_general(code_values, scaled_basis, (((0,), (0,)), ((), (...  147 us
    all_to_all x1, starting transfers between devices, per_device(): lax.all_to_all(jnp.stack([summed] * lax.axis_size('tm')), 'tm', 0, 0)  14.9 us
    dot_general x6, matrix products, highest(): jnp.dot(left_mat, right_mat, precision=lax.Precision.HIGHEST, preferred_e...  14 us
    all_to_all x1, waiting for transfers between devices, per_device(): lax.all_to_all(jnp.stack([summed] * lax.axis_size('tm')), 'tm', 0, 0)  12.3 us
    dot_general x4, matrix products, contract(): lax.dot_general(left_feats, right_feats, (((1,), (1,)), ((), ())), prefer...  6.4 us
  transfers between devices with their start and end apart: 2, of which 2 were waited for; matrix products, arithmetic and copies ran while one was open for 2% of the time, Pallas kernels for 0%

profile of v1, /device:TPU:1, one launch (start us, length us, event | category | flops | bytes accessed | tf_op | source)
XLA Modules:
  0.0 223.3 jit_solution(11627700104859935925)
XLA Ops:
  6.5 0.0 all-reduce.2.cloned.1.call-start
  6.5 3.6 %convolution_bitcast_fusion = f32[128,128]{0,1:T(8,128)} fusion(bf16[4096,128]{1,0:T(8,128)(2,1)} %param.17, s32[4096,128]{1,0:T(8,128)} %param.15, f32[4096]{0:T(1024)} %param.16), kind=kOutput, calls=%fused_computation.24 | convolution fusion | flops 136314880 | bytes 3227648 | tf_op jit(solution)/shard_map/dot_general | solution.py:71
  10.2 0.0 copy-start.1
  10.2 0.0 copy-start.2
  10.2 0.0 copy-start.3
  10.2 0.0 copy-start
  10.2 0.0 all-reduce.2.cloned.1.call-update
  10.2 0.9 fusion.50
  11.1 147.1 %all-reduce.2.cloned.1.call-done = f32[128,128]{0,1:T(8,128)} async-done(((f32[128,128]{0,1:T(8,128)}), f32[128,128]{0,1:T(8,128)}) %all-reduce.2.cloned.1.call-update) | async-done | bytes 65552 | tf_op jit(solution)/shard_map/psum | solution.py:70
  158.2 0.9 copy.22
  159.2 1.1 stack.2
  160.2 14.9 %all-to-all-start = ((f32[16,128,128]{2,1,0:T(8,128)}), f32[16,128,128]{2,1,0:T(8,128)S(1)}, u32[]{:S(2)}, u32[]{:S(2)}) async-start(f32[16,128,128]{2,1,0:T(8,128)} %stack.2), calls=%async_computation | async-start | bytes 2097152 | tf_op jit(solution)/shard_map/all_to_all | solution.py:78
  175.1 0.0 copy-done.1
  175.1 0.0 copy-done.2
  175.1 0.0 copy-done.3
  175.1 0.6 select_reduce_fusion
  175.7 0.9 fusion.49
  176.6 0.7 convert_subtract_fusion
  177.3 0.1 iota_compare_fusion.4
  177.4 0.1 iota_compare_fusion.3
  177.6 0.1 iota_compare_fusion.2
  177.7 0.3 compare_and_fusion
  178.0 0.0 copy-done
  178.0 0.6 fusion.48
  178.6 12.3 %all-to-all-done = f32[16,128,128]{2,1,0:T(8,128)S(1)} async-done(((f32[16,128,128]{2,1,0:T(8,128)}), f32[16,128,128]{2,1,0:T(8,128)S(1)}, u32[]{:S(2)}, u32[]{:S(2)}) %all-to-all-start) | async-done | bytes 1048608 | tf_op jit(solution)/shard_map/all_to_all | solution.py:78
  191.0 0.2 reduce-precision_convert_fusion
  191.1 0.8 fusion.17
  191.9 0.8 fusion.24
  192.7 0.8 fusion.31
  193.5 0.8 multiply_convert_fusion
  194.3 0.8 convolution_multiply_fusion.3
  195.1 0.8 multiply_convert_fusion.2
  195.9 1.9 fusion.1
  197.8 1.6 fusion.15
  199.4 1.9 fusion.39
  201.3 2.2 convolution_subtract_fusion.1
  203.5 0.8 multiply_convert_fusion.1
  204.3 1.9 fusion
  206.2 1.9 fusion.2
  208.1 1.5 convolution_subtract_fusion.2
  209.6 1.6 fusion.38
  211.2 5.2 %convolution_subtract_fusion = f32[524,524]{1,0:T(8,128)} fusion(f32[524,524]{1,0:T(8,128)S(1)} %fusion, f32[524,262]{0,1:T(8,128)S(1)} %fusion.38, f32[524,262]{0,1:T(8,128)S(1)} %fusion.15, f32[262,524]{1,0:T(8,128)S(1)} %convolution_subtract_fusion.2, f32[262,524]{1,0:T(8,128)S(1)} %slice.46), kind=kOutput, calls=%fused_computation.6 | convolution fusion | flops 1727357696 | bytes 4393216 | tf_op jit(solution)/shard_map/dot_general | solution.py:49
  (3 shorter events, 0.1 us)
Async XLA Ops:
  6.5 151.7 %all-reduce.2.cloned.1.call-start = ((), (), s32[]{:S(2)}) async-start(), calls=%async_computation.1 | async-start | bytes 131072 | tf_op jit(solution)/shard_map/psum | solution.py:70
  10.2 164.9 %copy-start.1 = (s32[128]{0:T(128)S(1)}, s32[128]{0:T(128)}, u32[]{:S(2)}) copy-start(s32[128]{0:T(128)} %constant.33.clone) | copy-start | bytes 1540
  10.2 164.9 %copy-start.2 = (s32[128]{0:T(128)S(1)}, s32[128]{0:T(128)}, u32[]{:S(2)}) copy-start(s32[128]{0:T(128)} %constant.32.clone) | copy-start | bytes 1540
  10.2 164.9 %copy-start.3 = (s32[128]{0:T(128)S(1)}, s32[128]{0:T(128)}, u32[]{:S(2)}) copy-start(s32[128]{0:T(128)} %constant.35) | copy-start | bytes 1540
  10.2 167.8 %copy-start = (f32[2,262,262]{2,0,1:T(2,128)S(1)}, f32[2,262,262]{2,0,1:T(2,128)}, u32[]{:S(2)}) copy-start(f32[2,262,262]{2,0,1:T(2,128)} %param.20) | copy-start | bytes 1647460
  160.2 30.7 %all-to-all-start = ((f32[16,128,128]{2,1,0:T(8,128)}), f32[16,128,128]{2,1,0:T(8,128)S(1)}, u32[]{:S(2)}, u32[]{:S(2)}) async-start(f32[16,128,128]{2,1,0:T(8,128)} %stack.2), calls=%async_computation | async-start | bytes 2097152 | tf_op jit(solution)/shard_map/all_to_all | solution.py:78
Sparse Core Ops, SparseCore 0:
  10.3 147.8 all-reduce.1
